TPU v7x, 32 devices: a whole 2x2x4 slice. The times are simulated.
32 devices in a mesh: dp: 2 (over y), ctx: 4 (over x, core), tensor: 4 (over z).
Axes of the slice: x: 2, y: 2, z: 4, core: 2. Of those that a mesh axis runs over, the one named last changes fastest.
Arguments:
- hidden: bfloat16 [4, 1024, 2048], P('dp', 'ctx'), may hold values from -6 to 6
- cotangent: bfloat16 [4, 1024, 2048], P('dp', 'ctx'), may hold values from -6 to 6
- segment_ids: int32 [4, 1024], P('dp', 'ctx'), may hold values from 0 to 5, never falling along the last dimension, each value on 1 to 800 neighbouring positions
- attn_gain: bfloat16 [2048], P(('dp', 'ctx')), may hold values from 0.5 to 1.5
- w_query: bfloat16 [2048, 2048], P(('dp', 'ctx'), 'tensor'), may hold values from -0.125 to 0.125
- key_matrix: bfloat16 [2048, 256], P(('dp', 'ctx'), 'tensor'), may hold values from -0.125 to 0.125
- value_matrix: bfloat16 [2048, 256], P(('dp', 'ctx'), 'tensor'), may hold values from -0.125 to 0.125
- w_out: bfloat16 [2048, 2048], P('tensor', ('dp', 'ctx')), may hold values from -1 to 1
- mlp_gain: bfloat16 [2048], P(('dp', 'ctx')), may hold values from 0.5 to 1.5
- w_gate: bfloat16 [2048, 5632], P(('dp', 'ctx'), 'tensor'), may hold values from -0.125 to 0.125
- w_up: bfloat16 [2048, 5632], P(('dp', 'ctx'), 'tensor'), may hold values from -0.125 to 0.125
- w_down: bfloat16 [5632, 2048], P('tensor', ('dp', 'ctx')), may hold values from -0.078125 to 0.078125
Outputs:
- layer_out: bfloat16 [4, 1024, 2048], P('dp', 'ctx')
- d_hidden: float32 [4, 1024, 2048], P('dp', 'ctx')
- grad_attn_gain: float32 [2048], P(('dp', 'ctx'))
- grad_query: float32 [2048, 2048], P(('dp', 'ctx'), 'tensor')
- grad_key: float32 [2048, 256], P(('dp', 'ctx'), 'tensor')
- grad_value: float32 [2048, 256], P(('dp', 'ctx'), 'tensor')
- grad_out: float32 [2048, 2048], P('tensor', ('dp', 'ctx'))
- grad_mlp_gain: float32 [2048], P(('dp', 'ctx'))
- grad_gate: float32 [2048, 5632], P(('dp', 'ctx'), 'tensor')
- grad_up: float32 [2048, 5632], P(('dp', 'ctx'), 'tensor')
- grad_down: float32 [5632, 2048], P('tensor', ('dp', 'ctx'))
Inputs may be any that keep to these rules, and one draw needn't show every extreme that they name: `segment_ids`: along each sequence the ids never fall, every id appears, each document holds 1 to 800 tokens, and one holds exactly 800.
All inputs are finite; a program needn't handle non-finite values.
Results may differ from a plain program's by a relative error of at most 0.013.
Values may be sent and summed in bfloat16 or wider, within the bound.
No kernel may reach another device: no remote copies, remote signals or barrier semaphores. Data moves between devices by JAX's collectives and lax.ppermute only.
A program may use at most 192 MiB of HBM per device.

v0:
```python
import jax
import jax.numpy as jnp
from jax import lax
from jax.sharding import PartitionSpec as P

MB = 2
EPSILON = 1e-05
THETA = 10000.0
NEG_FILL = -1e30


def inv_rms(values):
    return lax.rsqrt(jnp.mean(values * values, axis=-1, keepdims=True) + EPSILON)


def angles_for(positions, head_size):
    freq_index = jnp.arange(head_size // 2, dtype=jnp.float32)
    inverse = jnp.power(jnp.float32(THETA), -2.0 * freq_index / head_size)
    angle_table = positions.astype(jnp.float32)[:, None] * inverse[None, :]
    return (jnp.cos(angle_table), jnp.sin(angle_table))


def rotary(vectors, cosine, sine_table):
    half_size = vectors.shape[-1] // 2
    front_half = vectors[..., :half_size]
    back_half = vectors[..., half_size:]
    return jnp.concatenate(
        [
            front_half * cosine - back_half * sine_table,
            back_half * cosine + front_half * sine_table,
        ],
        axis=-1,
    )


def norm_back(grad_normed, source, inv_scale, gain_full):
    normalized = source * inv_scale
    scaled = grad_normed * gain_full
    middle = jnp.mean(scaled * normalized, axis=-1, keepdims=True)
    gain_term = jnp.sum(grad_normed * normalized, axis=(0, 1))
    return (inv_scale * (scaled - normalized * middle), gain_term)


def collect(shards):
    return (
        lax.all_gather(shards[0], ("dp", "ctx"), axis=0, tiled=True),
        lax.all_gather(shards[1], ("dp", "ctx"), axis=0, tiled=True),
        lax.all_gather(shards[2], ("dp", "ctx"), axis=0, tiled=True),
        lax.all_gather(shards[3], ("dp", "ctx"), axis=0, tiled=True),
        lax.all_gather(shards[4], ("dp", "ctx"), axis=1, tiled=True),
        lax.all_gather(shards[5], ("dp", "ctx"), axis=0, tiled=True),
        lax.all_gather(shards[6], ("dp", "ctx"), axis=0, tiled=True),
        lax.all_gather(shards[7], ("dp", "ctx"), axis=0, tiled=True),
        lax.all_gather(shards[8], ("dp", "ctx"), axis=1, tiled=True),
    )


def contract(left_side, right_side):
    return jnp.einsum("stc,stf->cf", left_side, right_side, preferred_element_type=jnp.float32)


def project_back(grad_rows, weight_full):
    return jnp.einsum("stf,cf->stc", grad_rows, weight_full, preferred_element_type=jnp.float32)


def per_device(
    hidden,
    cotangent,
    segment_ids,
    attn_gain,
    w_query,
    key_matrix,
    value_matrix,
    w_out,
    mlp_gain,
    w_gate,
    w_up,
    w_down,
):
    shards = (attn_gain, w_query, key_matrix, value_matrix, w_out, mlp_gain, w_gate, w_up, w_down)
    span_len = hidden.shape[1]
    model_width = hidden.shape[2]
    seq_count = hidden.shape[0] // MB
    head_size = key_matrix.shape[1]
    local_heads = w_query.shape[1] // head_size
    seq_len = span_len * lax.axis_size("ctx")
    score_scale = head_size ** (-0.5)
    positions_q = lax.axis_index("ctx") * span_len + jnp.arange(span_len, dtype=jnp.int32)
    positions_k = jnp.arange(seq_len, dtype=jnp.int32)
    cosine, sine_table = angles_for(positions_q, head_size)
    cos_heads = cosine[:, None, :]
    sin_heads = sine_table[:, None, :]
    causal = positions_q[:, None] >= positions_k[None, :]
    grad_list = [
        jnp.zeros((model_width,), jnp.float32),
        jnp.zeros((model_width, w_query.shape[1]), jnp.float32),
        jnp.zeros((model_width, key_matrix.shape[1]), jnp.float32),
        jnp.zeros((model_width, value_matrix.shape[1]), jnp.float32),
        jnp.zeros((w_out.shape[0], model_width), jnp.float32),
        jnp.zeros((model_width,), jnp.float32),
        jnp.zeros((model_width, w_gate.shape[1]), jnp.float32),
        jnp.zeros((model_width, w_up.shape[1]), jnp.float32),
        jnp.zeros((w_down.shape[0], model_width), jnp.float32),
    ]
    outputs = []
    input_grads = []
    for batch_index in range(MB):
        gathered = collect(shards)
        gain_one, query_w, key_w, value_w, out_w, gain_two, gate_w, up_w, down_w = gathered
        gain_one = gain_one.astype(jnp.float32)
        gain_two = gain_two.astype(jnp.float32)
        row_range = slice(batch_index * seq_count, (batch_index + 1) * seq_count)
        source = hidden[row_range].astype(jnp.float32)
        seg_local = segment_ids[row_range]
        inv_one = inv_rms(source)
        first_normalized = (source * inv_one * gain_one).astype(jnp.bfloat16)
        query_proj = jnp.dot(first_normalized, query_w, preferred_element_type=jnp.float32)
        projected_keys = jnp.dot(first_normalized, key_w, preferred_element_type=jnp.float32)
        projected_values = jnp.dot(first_normalized, value_w, preferred_element_type=jnp.float32)
        query_rows = rotary(
            query_proj.reshape(seq_count, span_len, local_heads, head_size), cos_heads, sin_heads
        ).astype(jnp.bfloat16)
        keys_local = rotary(projected_keys, cosine, sine_table).astype(jnp.bfloat16)
        values_local = projected_values.astype(jnp.bfloat16)
        keys_all, values_all, seg_all = (
            lax.all_gather(keys_local, "ctx", axis=1, tiled=True),
            lax.all_gather(values_local, "ctx", axis=1, tiled=True),
            lax.all_gather(seg_local.astype(jnp.bfloat16), "ctx", axis=1, tiled=True),
        )
        allowed = (seg_local[:, :, None] == seg_all.astype(jnp.int32)[:, None, :]) & causal[None]
        allowed = allowed[:, None]
        logits = (
            jnp.einsum("sqhd,skd->shqk", query_rows, keys_all, preferred_element_type=jnp.float32)
            * score_scale
        )
        logits = jnp.where(allowed, logits, NEG_FILL)
        row_peak = jnp.max(logits, axis=-1, keepdims=True)
        shifted = jnp.exp(logits - row_peak)
        totals = jnp.sum(shifted, axis=-1, keepdims=True)
        probs_low = (shifted / totals).astype(jnp.bfloat16)
        log_norm = row_peak + jnp.log(totals)
        heads_out = jnp.einsum(
            "shqk,skd->sqhd", probs_low, values_all, preferred_element_type=jnp.float32
        )
        heads_out = heads_out.reshape(seq_count, span_len, local_heads * head_size).astype(
            jnp.bfloat16
        )
        attn_out = lax.psum(jnp.dot(heads_out, out_w, preferred_element_type=jnp.float32), "tensor")
        residual = source + attn_out
        inv_two = inv_rms(residual)
        normed_two = (residual * inv_two * gain_two).astype(jnp.bfloat16)
        gate_pre = jnp.dot(normed_two, gate_w, preferred_element_type=jnp.float32)
        up_pre = jnp.dot(normed_two, up_w, preferred_element_type=jnp.float32)
        gate_sigmoid = jax.nn.sigmoid(gate_pre)
        silu_gate = gate_pre * gate_sigmoid
        activated = (silu_gate * up_pre).astype(jnp.bfloat16)
        mlp_out = lax.psum(
            jnp.dot(activated, down_w, preferred_element_type=jnp.float32).astype(jnp.bfloat16),
            "tensor",
        ).astype(jnp.float32)
        outputs.append((residual + mlp_out).astype(jnp.bfloat16))
        grad_top = cotangent[row_range]
        grad_list[8] = grad_list[8] + contract(activated, grad_top)
        d_act = project_back(grad_top, down_w)
        d_gate = (d_act * up_pre * gate_sigmoid * (1.0 + gate_pre * (1.0 - gate_sigmoid))).astype(
            jnp.bfloat16
        )
        d_up = (d_act * silu_gate).astype(jnp.bfloat16)
        grad_list[6] = grad_list[6] + contract(normed_two, d_gate)
        grad_list[7] = grad_list[7] + contract(normed_two, d_up)
        mlp_partial = project_back(d_gate, gate_w) + project_back(d_up, up_w)
        d_normed_two = lax.psum(mlp_partial, "tensor")
        d_norm_two, gain_term_two = norm_back(d_normed_two, residual, inv_two, gain_two)
        d_residual = grad_top.astype(jnp.float32) + d_norm_two
        d_residual_low = d_residual.astype(jnp.bfloat16)
        grad_list[5] = grad_list[5] + gain_term_two
        grad_list[4] = grad_list[4] + contract(heads_out, d_residual_low)
        d_heads = project_back(d_residual_low, out_w).astype(jnp.bfloat16)
        d_heads = d_heads.reshape(seq_count, span_len, local_heads, head_size)
        again = (
            jnp.einsum("sqhd,skd->shqk", query_rows, keys_all, preferred_element_type=jnp.float32)
            * score_scale
        )
        again = jnp.where(allowed, again, NEG_FILL)
        probs_again = jnp.exp(again - log_norm)
        probs_again_low = probs_again.astype(jnp.bfloat16)
        d_probs = jnp.einsum(
            "sqhd,skd->shqk", d_heads, values_all, preferred_element_type=jnp.float32
        )
        row_delta = jnp.sum(probs_again * d_probs, axis=-1, keepdims=True)
        d_scores = (probs_again * (d_probs - row_delta)).astype(jnp.bfloat16)
        d_query = (
            jnp.einsum("shqk,skd->sqhd", d_scores, keys_all, preferred_element_type=jnp.float32)
            * score_scale
        )
        key_terms = (
            jnp.einsum("shqk,sqhd->ksd", d_scores, query_rows, preferred_element_type=jnp.float32)
            * score_scale
        )
        value_terms = jnp.einsum(
            "shqk,sqhd->ksd", probs_again_low, d_heads, preferred_element_type=jnp.float32
        )
        kv_terms = jnp.stack([key_terms, value_terms], axis=1).reshape(
            seq_len, 2 * seq_count * head_size
        )
        kv_local = lax.psum_scatter(kv_terms, "ctx", scatter_dimension=0, tiled=True).reshape(
            span_len, 2, seq_count, head_size
        )
        d_key = jnp.transpose(kv_local[:, 0], (1, 0, 2))
        d_value = jnp.transpose(kv_local[:, 1], (1, 0, 2))
        d_query_proj = rotary(d_query, cos_heads, -sin_heads).astype(jnp.bfloat16)
        d_query_proj = d_query_proj.reshape(seq_count, span_len, local_heads * head_size)
        d_key_proj = rotary(d_key, cosine, -sine_table).astype(jnp.bfloat16)
        d_value_proj = d_value.astype(jnp.bfloat16)
        grad_list[1] = grad_list[1] + contract(first_normalized, d_query_proj)
        grad_list[2] = grad_list[2] + contract(first_normalized, d_key_proj)
        grad_list[3] = grad_list[3] + contract(first_normalized, d_value_proj)
        attn_partial = (
            project_back(d_query_proj, query_w)
            + project_back(d_key_proj, key_w)
            + project_back(d_value_proj, value_w)
        )
        d_normed_one = lax.psum(attn_partial, "tensor")
        d_norm_one, gain_term_one = norm_back(d_normed_one, source, inv_one, gain_one)
        grad_list[0] = grad_list[0] + gain_term_one
        input_grads.append(d_residual + d_norm_one)
    input_grad_rows = jnp.concatenate(input_grads, axis=0)
    summed = (
        lax.psum_scatter(grad_list[0], ("dp", "ctx"), scatter_dimension=0, tiled=True),
        lax.psum_scatter(grad_list[1], ("dp", "ctx"), scatter_dimension=0, tiled=True),
        lax.psum_scatter(grad_list[2], ("dp", "ctx"), scatter_dimension=0, tiled=True),
        lax.psum_scatter(grad_list[3], ("dp", "ctx"), scatter_dimension=0, tiled=True),
        lax.psum_scatter(grad_list[4], ("dp", "ctx"), scatter_dimension=1, tiled=True),
        lax.psum_scatter(grad_list[5], ("dp", "ctx"), scatter_dimension=0, tiled=True),
        lax.psum_scatter(grad_list[6], ("dp", "ctx"), scatter_dimension=0, tiled=True),
        lax.psum_scatter(grad_list[7], ("dp", "ctx"), scatter_dimension=0, tiled=True),
        lax.psum_scatter(grad_list[8], ("dp", "ctx"), scatter_dimension=1, tiled=True),
    )
    return (
        jnp.concatenate(outputs, axis=0),
        input_grad_rows,
        summed[0],
        summed[1],
        summed[2],
        summed[3],
        summed[4],
        summed[5],
        summed[6],
        summed[7],
        summed[8],
    )


def solution(mesh):
    in_specs = (
        P("dp", "ctx", None),
        P("dp", "ctx", None),
        P("dp", "ctx"),
        P(("dp", "ctx")),
        P(("dp", "ctx"), "tensor"),
        P(("dp", "ctx"), "tensor"),
        P(("dp", "ctx"), "tensor"),
        P("tensor", ("dp", "ctx")),
        P(("dp", "ctx")),
        P(("dp", "ctx"), "tensor"),
        P(("dp", "ctx"), "tensor"),
        P("tensor", ("dp", "ctx")),
    )
    out_specs = (
        P("dp", "ctx", None),
        P("dp", "ctx", None),
        P(("dp", "ctx")),
        P(("dp", "ctx"), "tensor"),
        P(("dp", "ctx"), "tensor"),
        P(("dp", "ctx"), "tensor"),
        P("tensor", ("dp", "ctx")),
        P(("dp", "ctx")),
        P(("dp", "ctx"), "tensor"),
        P(("dp", "ctx"), "tensor"),
        P("tensor", ("dp", "ctx")),
    )
    return jax.shard_map(
        per_device, mesh=mesh, in_specs=in_specs, out_specs=out_specs, check_vma=False
    )
```

profile of v0, /device:TPU:0, one launch (start us, length us, event | category | flops | bytes accessed | tf_op | source)
XLA Modules:
  0.0 1380.9 jit_solution(2608815866896692798)
XLA Ops:
  11.5 10.4 all-gather.2
  22.0 9.8 all_gather.58
  32.9 9.8 all_gather.55
  43.7 5.1 all_gather.57
  48.7 5.1 all_gather.67
  54.9 5.4 all_gather.68
  60.3 6.0 all_gather.59
  66.3 5.4 all-gather
  71.7 6.1 all-gather.1
  78.5 3.9 copy.47
  82.4 2.6 convolution_bitcast_fusion.2
  95.2 3.8 convolution_bitcast_fusion.1
  99.0 2.0 convolution_bitcast_fusion
  102.9 9.4 all-gather.3
  112.3 144.4 %all-reduce.16.cloned.1.call-done = (f32[1,256,2048]{2,1,0:T(8,128)}, f32[1,256,2048]{2,1,0:T(8,128)}) async-done(((f32[1,256,2048]{2,1,0:T(8,128)}, f32[1,256,2048]{2,1,0:T(8,128)}), (f32[1,256,2048]{2,1,0:T(8,128)}, f32[1,256,2048]{2,1,0:T(8,128)})) %all-reduce.16.cloned.1.call-update) | async-done | bytes 4194320 | tf_op jit(solution)/shard_map/psum | solution.py:148
  256.7 2.8 multiply_reduce_fusion.5
  262.9 37.8 %all-gather.16.cloned.1.call-done = bf16[2048,1408]{1,0:T(8,128)(2,1)} async-done(((bf16[256,1408]{1,0:T(8,128)(2,1)}), bf16[2048,1408]{1,0:T(8,128)(2,1)}) %all-gather.16.cloned.1.call-update) | async-done | bytes 5767184 | tf_op jit(solution)/shard_map/all_gather | solution.py:53
  300.6 5.9 fusion.193
  306.5 39.1 %all-gather.14.cloned.1.call-done = bf16[2048,1408]{1,0:T(8,128)(2,1)} async-done(((bf16[256,1408]{1,0:T(8,128)(2,1)}), bf16[2048,1408]{1,0:T(8,128)(2,1)}) %all-gather.14.cloned.1.call-update) | async-done | bytes 5767184 | tf_op jit(solution)/shard_map/all_gather | solution.py:52
  345.6 6.0 fusion.192
  351.6 2.9 fusion.195
  354.5 2.9 fusion.194
  357.5 34.2 %all-gather.18.cloned.1.call-done = bf16[1408,2048]{1,0:T(8,128)(2,1)} async-done(((bf16[1408,256]{1,0:T(8,128)(2,1)}), bf16[1408,2048]{1,0:T(8,128)(2,1)}) %all-gather.18.cloned.1.call-update) | async-done | bytes 5767184 | tf_op jit(solution)/shard_map/all_gather | solution.py:54
  391.6 7.1 multiply_convert_fusion.2
  399.6 4.6 fusion.198
  404.5 3.7 multiply_convert_fusion.4
  410.1 3.1 fusion.35
  413.3 3.1 fusion.34
  416.5 5.7 fusion.36
  422.2 5.7 fusion.37
  429.2 142.4 %all-reduce.14.cloned.1.call-done = (f32[1,256,2048]{2,1,0:T(8,128)}, f32[1,256,2048]{2,1,0:T(8,128)}) async-done(((f32[1,256,2048]{2,1,0:T(8,128)}, f32[1,256,2048]{2,1,0:T(8,128)}), (f32[1,256,2048]{2,1,0:T(8,128)}, f32[1,256,2048]{2,1,0:T(8,128)})) %all-reduce.14.cloned.1.call-update) | async-done | bytes 4194320 | tf_op jit(solution)/shard_map/psum | solution.py:172
  571.6 5.0 multiply_reduce_fusion.1
  576.6 83.1 %all-reduce.18.cloned.1.call-done = (bf16[1,256,2048]{2,1,0:T(8,128)(2,1)}, bf16[1,256,2048]{2,1,0:T(8,128)(2,1)}) async-done(((bf16[1,256,2048]{2,1,0:T(8,128)(2,1)}, bf16[1,256,2048]{2,1,0:T(8,128)(2,1)}), (bf16[1,256,2048]{2,1,0:T(8,128)(2,1)}, bf16[1,256,2048]{2,1,0:T(8,128)(2,1)})) %all-reduce.18.cloned.1.call-update) | async-done | bytes 2097168 | tf_op jit(solution)/shard_map/psum | solution.py:157
  659.8 7.3 multiply_add_fusion.1
  671.0 5.5 fusion.65
  676.6 8.8 fusion
  688.0 5.7 fusion.62
  693.6 8.9 fusion.3
  707.5 7.0 fusion.16
  722.1 2.1 fusion.199
  724.2 2.1 fusion.197
  728.9 23.7 %reduce-scatter.10.cloned.1.call-done = f32[256,128]{0,1:T(8,128)} async-done(((f32[1024,128]{0,1:T(8,128)}), f32[256,128]{0,1:T(8,128)}) %reduce-scatter.10.cloned.1.call-update) | async-done | bytes 131088 | tf_op jit(solution)/shard_map/reduce_scatter | solution.py:206
  754.4 2.1 convolution_add_fusion.6
  766.5 2.8 fusion.79
  769.3 2.7 convolution_add_fusion.3
  773.9 2.9 convolution_add_fusion.4
  777.1 3.3 fusion.201
  780.4 6.1 convolution_add_fusion.1
  786.7 3.3 fusion.200
  790.0 6.1 convolution_add_fusion.2
  797.2 3.1 fusion.82
  800.3 5.9 convolution_add_fusion
  808.1 2.7 pad_maximum_fusion.1
  810.9 105.5 %all-reduce.12.cloned.1.call-done = (f32[1,256,2048]{2,1,0:T(8,128)}, f32[1,256,2048]{2,1,0:T(8,128)}) async-done(((f32[1,256,2048]{2,1,0:T(8,128)}, f32[1,256,2048]{2,1,0:T(8,128)}), (f32[1,256,2048]{2,1,0:T(8,128)}, f32[1,256,2048]{2,1,0:T(8,128)})) %all-reduce.12.cloned.1.call-update) | async-done | bytes 4194320 | tf_op jit(solution)/shard_map/psum | solution.py:223
  916.4 3.3 fusion.43
  919.7 23.9 %all-reduce.2 = (f32[2048]{0:T(1024)S(1)}, f32[2048]{0:T(1024)S(1)}) all-reduce(f32[2048]{0:T(1024)S(1)} %add.260, f32[2048]{0:T(1024)S(1)} %add.265), channel_id=6, replica_groups=mesh['dp'=2,'ctx'=4,'tensor'=4] {'dp','ctx'}, use_global_device_ids=true, to_apply=%region_26.27.clone | all-reduce | flops 4096 | bytes 32768
  944.9 4.5 fusion.42
  949.4 2.5 pad_maximum_fusion
  953.0 37.8 %reduce-scatter.18.cloned.1.call-done = f32[256,64]{0,1:T(8,128)} async-done(((f32[2048,64]{0,1:T(8,128)}), f32[256,64]{0,1:T(8,128)}) %reduce-scatter.18.cloned.1.call-update) | async-done | bytes 65552 | tf_op jit(solution)/shard_map/reduce_scatter | solution.py:232
  990.8 54.9 %reduce-scatter.20.cloned.1.call-done = f32[512,256]{1,0:T(8,128)} async-done(((f32[512,2048]{1,0:T(8,128)}), f32[512,256]{1,0:T(8,128)}) %reduce-scatter.20.cloned.1.call-update) | async-done | bytes 524304 | tf_op jit(solution)/shard_map/reduce_scatter | solution.py:233
  1045.7 55.0 %reduce-scatter.14.cloned.1.call-done = f32[256,512]{1,0:T(8,128)} async-done(((f32[2048,512]{1,0:T(8,128)}), f32[256,512]{1,0:T(8,128)}) %reduce-scatter.14.cloned.1.call-update) | async-done | bytes 524304 | tf_op jit(solution)/shard_map/reduce_scatter | solution.py:230
  1100.7 91.1 %reduce-scatter.24.cloned.1.call-done = f32[256,1408]{1,0:T(8,128)} async-done(((f32[2048,1408]{1,0:T(8,128)}), f32[256,1408]{1,0:T(8,128)}) %reduce-scatter.24.cloned.1.call-update) | async-done | bytes 1441808 | tf_op jit(solution)/shard_map/reduce_scatter | solution.py:236
  1191.8 91.1 %reduce-scatter.22.cloned.1.call-done = f32[256,1408]{1,0:T(8,128)} async-done(((f32[2048,1408]{1,0:T(8,128)}), f32[256,1408]{1,0:T(8,128)}) %reduce-scatter.22.cloned.1.call-update) | async-done | bytes 1441808 | tf_op jit(solution)/shard_map/reduce_scatter | solution.py:235
  1282.9 90.8 %reduce-scatter.26.cloned.1.call-done = f32[1408,256]{1,0:T(8,128)} async-done(((f32[1408,2048]{1,0:T(8,128)}), f32[1408,256]{1,0:T(8,128)}) %reduce-scatter.26.cloned.1.call-update) | async-done | bytes 1441808 | tf_op jit(solution)/shard_map/reduce_scatter | solution.py:237
  (322 shorter events, 67.3 us)
Async XLA Ops:
  7.2 24.6 %copy-start.2 = (bf16[2,256,2048]{2,1,0:T(8,128)(2,1)S(1)}, bf16[2,256,2048]{2,1,0:T(8,128)(2,1)}, u32[]{:S(2)}) copy-start(bf16[2,256,2048]{2,1,0:T(8,128)(2,1)} %param.12) | copy-start | bytes 6291460
  7.2 14.8 %copy-start.77 = (bf16[256,64]{0,1:T(8,128)(2,1)S(1)}, bf16[256,64]{0,1:T(8,128)(2,1)}, u32[]{:S(2)}) copy-start(bf16[256,64]{0,1:T(8,128)(2,1)} %param.17) | copy-start | bytes 98308
  7.2 71.3 %all-gather.10.cloned.1.call-start = ((), (), s32[]{:S(2)}) async-start(), calls=%async_computation.9 | async-start | bytes 2359296 | tf_op jit(solution)/shard_map/all_gather | solution.py:47
  7.9 87.2 %all-gather.12.cloned.1.call-start = ((), (), s32[]{:S(2)}) async-start(), calls=%async_computation.10 | async-start | bytes 2359296 | tf_op jit(solution)/shard_map/all_gather | solution.py:50
  8.7 248.0 %all-reduce.16.cloned.1.call-start = ((), (), s32[]{:S(2)}) async-start(), calls=%async_computation.25 | async-start | bytes 8388608 | tf_op jit(solution)/shard_map/psum | solution.py:148
  8.7 45.9 %copy-start.85 = (f32[32]{0:T(128)}, f32[32]{0:T(128)S(1)}, u32[]{:S(2)}) copy-start(f32[32]{0:T(128)S(1)} %multiply_power_fusion) | copy-start | bytes 388
  8.8 45.9 %copy-start.83 = (f32[256]{0:T(256)}, f32[256]{0:T(256)S(1)}, u32[]{:S(2)}) copy-start(f32[256]{0:T(256)S(1)} %fusion.169) | copy-start | bytes 3076
  11.5 73.5 %copy-start.79 = (f32[256]{0:T(256)}, f32[256]{0:T(256)S(1)}, u32[]{:S(2)}) copy-start(f32[256]{0:T(256)S(1)} %add_rsqrt_fusion.3) | copy-start | bytes 3076
  11.5 70.9 %copy-start.81 = (f32[256]{0:T(256)}, f32[256]{0:T(256)S(1)}, u32[]{:S(2)}) copy-start(f32[256]{0:T(256)S(1)} %add_rsqrt_fusion.1) | copy-start | bytes 3076
  66.3 19.8 %copy-start.29 = (bf16[1,1024,64]{1,2,0:T(8,128)(2,1)}, bf16[1,1024,64]{1,2,0:T(8,128)(2,1)S(1)}, u32[]{:S(2)}) copy-start(bf16[1,1024,64]{1,2,0:T(8,128)(2,1)S(1)} %all_gather.59) | copy-start | bytes 393220
  71.7 19.5 %copy-start.52 = (bf16[1024,64]{0,1:T(8,128)(2,1)}, bf16[1024,64]{0,1:T(8,128)(2,1)S(1)}, u32[]{:S(2)}) copy-start(bf16[1024,64]{0,1:T(8,128)(2,1)S(1)} %all-gather) | copy-start | bytes 393220
  87.5 3.7 copy-start
  87.5 3.7 copy-start.64
  88.9 4.7 copy-start.1
  95.1 3.8 copy-start.43
  95.2 3.8 copy-start.7
  101.1 199.6 %all-gather.16.cloned.1.call-start = ((), (), s32[]{:S(2)}) async-start(), calls=%async_computation.12 | async-start | bytes 6488064 | tf_op jit(solution)/shard_map/all_gather | solution.py:53
  101.6 243.9 %all-gather.14.cloned.1.call-start = ((), (), s32[]{:S(2)}) async-start(), calls=%async_computation.11 | async-start | bytes 6488064 | tf_op jit(solution)/shard_map/all_gather | solution.py:52
  102.2 289.4 %all-gather.18.cloned.1.call-start = ((), (), s32[]{:S(2)}) async-start(), calls=%async_computation.13 | async-start | bytes 6488064 | tf_op jit(solution)/shard_map/all_gather | solution.py:54
  102.8 468.8 %all-reduce.14.cloned.1.call-start = ((), (), s32[]{:S(2)}) async-start(), calls=%async_computation.24 | async-start | bytes 8388608 | tf_op jit(solution)/shard_map/psum | solution.py:172
  345.6 6.0 copy-start.89
  345.6 8.9 slice-start.6
  391.6 12.6 copy-start.92
  391.6 12.6 copy-start.93
  398.7 14.6 %copy-start.50 = (bf16[256,1408]{1,0:T(8,128)(2,1)}, bf16[256,1408]{1,0:T(8,128)(2,1)S(1)}, u32[]{:S(2)}) copy-start(bf16[256,1408]{1,0:T(8,128)(2,1)S(1)} %get-tuple-element.40) | copy-start | bytes 2162692
  399.6 4.7 copy-start.14
  399.6 5.0 copy-start.88
  399.6 8.7 slice-start.8
  399.6 10.5 slice-start.4
  404.5 3.7 slice-start.9
  404.5 5.6 slice-start.5
  416.5 243.3 %all-reduce.18.cloned.1.call-start = ((), (), s32[]{:S(2)}) async-start(), calls=%async_computation.26 | async-start | bytes 4194304 | tf_op jit(solution)/shard_map/psum | solution.py:157
  416.5 5.7 copy-start.18
  427.9 300.2 %reduce-scatter.12.cloned.1.call-start = ((), (), s32[]{:S(2)}) async-start(), calls=%async_computation.15 | async-start | bytes 655360 | tf_op jit(solution)/shard_map/reduce_scatter | solution.py:206
  659.8 8.7 copy-start.8
  671.0 5.6 copy-start.55
  671.0 5.5 copy-start.58
  676.6 8.8 copy-start.9
  676.6 8.8 copy-start.10
  687.9 5.7 copy-start.53
  688.0 14.6 %slice-start = ((s8[8388608]{0:T(1024)(128)(4,1)}), s8[4194304]{0:T(1024)(128)(4,1)S(1)}, s32[]{:S(2)}) async-start(s8[8388608]{0:T(1024)(128)(4,1)} %bitcast.333), calls=%async_computation.27 | async-start | bytes 8388608
  688.0 14.6 %slice-start.2 = ((s8[8388608]{0:T(1024)(128)(4,1)}), s8[4194304]{0:T(1024)(128)(4,1)S(1)}, s32[]{:S(2)}) async-start(s8[8388608]{0:T(1024)(128)(4,1)} %bitcast.335), calls=%async_computation.29 | async-start | bytes 8388608
  693.6 9.0 slice-start.1
  693.6 9.0 slice-start.3
  693.6 9.0 copy-start.59
  693.6 9.0 copy-start.74
  707.2 45.4 %reduce-scatter.10.cloned.1.call-start = ((), (), s32[]{:S(2)}) async-start(), calls=%async_computation.14 | async-start | bytes 655360 | tf_op jit(solution)/shard_map/reduce_scatter | solution.py:206
  707.5 7.0 copy-start.32
  707.5 7.0 copy-start.34
  720.1 196.2 %all-reduce.12.cloned.1.call-start = ((), (), s32[]{:S(2)}) async-start(), calls=%async_computation.23 | async-start | bytes 8388608 | tf_op jit(solution)/shard_map/psum | solution.py:223
  724.2 29.3 %copy-start.84 = (f32[256]{0:T(256)S(1)}, f32[256]{0:T(256)}, u32[]{:S(2)}) copy-start(f32[256]{0:T(256)} %copy-done.83) | copy-start | bytes 3076
  724.2 29.3 %copy-start.86 = (f32[32]{0:T(128)S(1)}, f32[32]{0:T(128)}, u32[]{:S(2)}) copy-start(f32[32]{0:T(128)} %copy-done.85) | copy-start | bytes 388
  724.2 30.2 %copy-start.21 = (bf16[2048,64]{0,1:T(8,128)(2,1)S(1)}, bf16[2048,64]{0,1:T(8,128)(2,1)}, u32[]{:S(2)}) copy-start(bf16[2048,64]{0,1:T(8,128)(2,1)} %copy-done.20) | copy-start | bytes 786436
  753.8 4.5 copy-start.70
  753.8 4.5 copy-start.72
  761.2 191.8 %reduce-scatter.16.cloned.1.call-start = ((), (), s32[]{:S(2)}) async-start(), calls=%async_computation.17 | async-start | bytes 589824 | tf_op jit(solution)/shard_map/reduce_scatter | solution.py:231
  763.7 227.1 %reduce-scatter.18.cloned.1.call-start = ((), (), s32[]{:S(2)}) async-start(), calls=%async_computation.18 | async-start | bytes 589824 | tf_op jit(solution)/shard_map/reduce_scatter | solution.py:232
  766.4 279.3 %reduce-scatter.20.cloned.1.call-start = ((), (), s32[]{:S(2)}) async-start(), calls=%async_computation.19 | async-start | bytes 4718592 | tf_op jit(solution)/shard_map/reduce_scatter | solution.py:233
  772.0 328.7 %reduce-scatter.14.cloned.1.call-start = ((), (), s32[]{:S(2)}) async-start(), calls=%async_computation.16 | async-start | bytes 4718592 | tf_op jit(solution)/shard_map/reduce_scatter | solution.py:230
  776.8 415.0 %reduce-scatter.24.cloned.1.call-start = ((), (), s32[]{:S(2)}) async-start(), calls=%async_computation.21 | async-start | bytes 12976128 | tf_op jit(solution)/shard_map/reduce_scatter | solution.py:236
  777.1 3.3 copy-start.51
  786.6 496.3 %reduce-scatter.22.cloned.1.call-start = ((), (), s32[]{:S(2)}) async-start(), calls=%async_computation.20 | async-start | bytes 12976128 | tf_op jit(solution)/shard_map/reduce_scatter | solution.py:235
  796.1 4.2 copy-start.19
  796.1 577.5 %reduce-scatter.26.cloned.1.call-start = ((), (), s32[]{:S(2)}) async-start(), calls=%async_computation.22 | async-start | bytes 12976128 | tf_op jit(solution)/shard_map/reduce_scatter | solution.py:237
  (58 other events, 94.0 us)
Sparse Core Ops, SparseCore 0:
  9.9 31.1 all-gather.9
  43.0 28.4 all-gather.11
  101.2 155.4 all-reduce.15
  258.4 42.1 all-gather.15
  302.4 43.1 all-gather.13
  347.3 44.2 all-gather.17
  416.6 154.9 all-reduce.13
  574.6 85.1 all-reduce.17
  707.4 20.6 reduce-scatter.11
  731.0 21.6 reduce-scatter.9
  761.3 155.0 all-reduce.11
  919.9 33.0 reduce-scatter.15
  956.6 34.1 reduce-scatter.17
  994.6 51.0 reduce-scatter.19
  1049.5 51.1 reduce-scatter.13
  1104.6 87.1 reduce-scatter.23
  1195.7 87.1 reduce-scatter.21
  1286.8 86.8 reduce-scatter.25
where the time goes:
time: 1390 us; the launch traced here: 1380 us
  waiting for transfers between devices  1040 us (75%)
  matrix products  159 us (11%)
  blocking collectives  96.4 us (7%)
  other arithmetic  48.5 us (3%)
  local copies, waits for them, and re-layouts  21.8 us (2%)
  between operations  16.7 us (1%)
    psum x1, waiting for transfers between devices, per_device(): lax.psum(jnp.dot(heads_out, out_w, preferred_element_type=jnp.float32), '...  144 us
    psum x1, waiting for transfers between devices, per_device(): d_normed_two = lax.psum(mlp_partial, 'tensor')  142 us
    psum x1, waiting for transfers between devices, per_device(): d_normed_one = lax.psum(attn_partial, 'tensor')  106 us
    reduce_scatter x1, waiting for transfers between devices, per_device(): lax.psum_scatter(grad_list[7], ('dp', 'ctx'), scatter_dimension=0, tiled=...  91.1 us
    reduce_scatter x1, waiting for transfers between devices, per_device(): lax.psum_scatter(grad_list[6], ('dp', 'ctx'), scatter_dimension=0, tiled=...  91.1 us
    reduce_scatter x1, waiting for transfers between devices, per_device(): lax.psum_scatter(grad_list[8], ('dp', 'ctx'), scatter_dimension=1, tiled=...  90.8 us
    psum x1, waiting for transfers between devices, per_device(): lax.psum(jnp.dot(activated, down_w, preferred_element_type=jnp.float32).a...  83.1 us
    reduce_scatter x1, waiting for transfers between devices, per_device(): lax.psum_scatter(grad_list[1], ('dp', 'ctx'), scatter_dimension=0, tiled=...  55 us
  transfers between devices with their start and end apart: 18, of which 16 were waited for; matrix products, arithmetic and copies ran while one was open for 10% of the time, Pallas kernels for 0%

commit v1 on v0

--- a/solution.py
+++ b/solution.py
@@ -169,7 +169,11 @@
         grad_list[6] = grad_list[6] + contract(normed_two, d_gate)
         grad_list[7] = grad_list[7] + contract(normed_two, d_up)
         mlp_partial = project_back(d_gate, gate_w) + project_back(d_up, up_w)
-        d_normed_two = lax.psum(mlp_partial, "tensor")
+        d_normed_two = mlp_partial
+        for hop in (1, 2):
+            d_normed_two = d_normed_two + lax.ppermute(
+                d_normed_two, "tensor", [(dev, dev ^ hop) for dev in range(4)]
+            )
         d_norm_two, gain_term_two = norm_back(d_normed_two, residual, inv_two, gain_two)
         d_residual = grad_top.astype(jnp.float32) + d_norm_two
         d_residual_low = d_residual.astype(jnp.bfloat16)

time: 1390 us -> 1500 us (1.079)
  waiting for transfers between devices: 1040 us -> 1150 us
  matrix products: 159 us -> 143 us
    ppermute x0 -> x4, waiting for transfers between devices: none -> 333 us  [per_device(): lax.ppermute(d_normed_two, 'tensor', [(dev, dev ^ hop) for dev in range(4)])]
    psum x1 -> x0, waiting for transfers between devices: 142 us -> none  [per_device(): d_normed_two = lax.psum(mlp_partial, 'tensor')]
    psum x1, waiting for transfers between devices: 83.1 us -> 0.01 us  [per_device(): lax.psum(jnp.dot(activated, down_w, preferred_element_type=jnp.float32).a...]
  transfers between devices with their start and end apart: 18 -> 21, of which waited for: 16 -> 18; matrix products, arithmetic and copies ran while one was open for 10% -> 8% of each run, Pallas kernels for 0% -> 0%
where the time goes in v1:
time: 1500 us
  waiting for transfers between devices  1150 us (77%)
  matrix products  143 us (10%)
  blocking collectives  96.6 us (6%)
  other arithmetic  58.1 us (4%)
  local copies, waits for them, and re-layouts  21 us (1%)
  between operations  16.2 us (1%)
    ppermute x4, waiting for transfers between devices, per_device(): lax.ppermute(d_normed_two, 'tensor', [(dev, dev ^ hop) for dev in range(4)])  333 us
    psum x1, waiting for transfers between devices, per_device(): lax.psum(jnp.dot(heads_out, out_w, preferred_element_type=jnp.float32), '...  144 us
    psum x1, waiting for transfers between devices, per_device(): d_normed_one = lax.psum(attn_partial, 'tensor')  106 us
    reduce_scatter x1, waiting for transfers between devices, per_device(): lax.psum_scatter(grad_list[7], ('dp', 'ctx'), scatter_dimension=0, tiled=...  91.1 us
    reduce_scatter x1, waiting for transfers between devices, per_device(): lax.psum_scatter(grad_list[6], ('dp', 'ctx'), scatter_dimension=0, tiled=...  91.1 us
    reduce_scatter x1, waiting for transfers between devices, per_device(): lax.psum_scatter(grad_list[8], ('dp', 'ctx'), scatter_dimension=1, tiled=...  90.8 us
    reduce_scatter x1, waiting for transfers between devices, per_device(): lax.psum_scatter(grad_list[1], ('dp', 'ctx'), scatter_dimension=0, tiled=...  55.1 us
    reduce_scatter x1, waiting for transfers between devices, per_device(): lax.psum_scatter(grad_list[4], ('dp', 'ctx'), scatter_dimension=1, tiled=...  54.9 us
  transfers between devices with their start and end apart: 21, of which 18 were waited for; matrix products, arithmetic and copies ran while one was open for 8% of the time, Pallas kernels for 0%

profile of v1, /device:TPU:0, one launch (start us, length us, event | category | flops | bytes accessed | tf_op | source)
XLA Modules:
  0.0 1496.5 jit_solution(17346873056342966282)
XLA Ops:
  9.5 10.4 all-gather.2
  19.9 2.1 fusion.44
  22.0 9.8 all_gather.58
  32.9 9.8 all_gather.55
  44.8 5.4 all_gather.68
  50.2 5.1 all_gather.57
  55.3 5.1 all_gather.67
  60.3 6.1 all-gather.1
  66.4 5.5 all_gather.59
  71.9 6.3 all-gather
  78.9 3.9 copy.47
  82.9 2.6 convolution_bitcast_fusion.3
  95.6 3.8 convolution_bitcast_fusion
  103.3 9.3 all-gather.3
  112.6 144.4 %all-reduce.12.cloned.1.call-done = (f32[1,256,2048]{2,1,0:T(8,128)}, f32[1,256,2048]{2,1,0:T(8,128)}) async-done(((f32[1,256,2048]{2,1,0:T(8,128)}, f32[1,256,2048]{2,1,0:T(8,128)}), (f32[1,256,2048]{2,1,0:T(8,128)}, f32[1,256,2048]{2,1,0:T(8,128)})) %all-reduce.12.cloned.1.call-update) | async-done | bytes 4194320 | tf_op jit(solution)/shard_map/psum | solution.py:148
  257.1 4.1 multiply_reduce_fusion.5
  262.7 38.3 %all-gather.14.cloned.1.call-done = bf16[2048,1408]{1,0:T(8,128)(2,1)} async-done(((bf16[256,1408]{1,0:T(8,128)(2,1)}), bf16[2048,1408]{1,0:T(8,128)(2,1)}) %all-gather.14.cloned.1.call-update) | async-done | bytes 5767184 | tf_op jit(solution)/shard_map/all_gather | solution.py:52
  301.0 5.5 fusion.192
  306.5 39.4 %all-gather.16.cloned.1.call-done = bf16[2048,1408]{1,0:T(8,128)(2,1)} async-done(((bf16[256,1408]{1,0:T(8,128)(2,1)}), bf16[2048,1408]{1,0:T(8,128)(2,1)}) %all-gather.16.cloned.1.call-update) | async-done | bytes 5767184 | tf_op jit(solution)/shard_map/all_gather | solution.py:53
  345.9 5.5 fusion.193
  351.5 40.5 %all-gather.18.cloned.1.call-done = bf16[1408,2048]{1,0:T(8,128)(2,1)} async-done(((bf16[1408,256]{1,0:T(8,128)(2,1)}), bf16[1408,2048]{1,0:T(8,128)(2,1)}) %all-gather.18.cloned.1.call-update) | async-done | bytes 5767184 | tf_op jit(solution)/shard_map/all_gather | solution.py:54
  392.0 6.2 multiply_convert_fusion.4
  405.0 46.3 %collective-permute-done = f32[1,256,2048]{2,1,0:T(8,128)S(1)} collective-permute-done((f32[1,256,2048]{2,1,0:T(8,128)S(1)}, f32[1,256,2048]{2,1,0:T(8,128)S(1)}, u32[]{:S(2)}, u32[]{:S(2)}) %collective-permute-start) | collective-permute-done | bytes 2097184 | tf_op jit(solution)/shard_map/ppermute | solution.py:174
  451.6 2.5 collective-permute-start.1
  455.9 88.5 %collective-permute-done.1 = f32[1,256,2048]{2,1,0:T(8,128)S(1)} collective-permute-done((f32[1,256,2048]{2,1,0:T(8,128)S(1)}, f32[1,256,2048]{2,1,0:T(8,128)S(1)}, u32[]{:S(2)}, u32[]{:S(2)}) %collective-permute-start.1) | collective-permute-done | bytes 2097184 | tf_op jit(solution)/shard_map/ppermute | solution.py:174
  547.8 2.4 multiply_convert_fusion.2
  554.5 46.1 %collective-permute-done.2 = f32[1,256,2048]{2,1,0:T(8,128)S(1)} collective-permute-done((f32[1,256,2048]{2,1,0:T(8,128)S(1)}, f32[1,256,2048]{2,1,0:T(8,128)S(1)}, u32[]{:S(2)}, u32[]{:S(2)}) %collective-permute-start.2) | collective-permute-done | bytes 2097184 | tf_op jit(solution)/shard_map/ppermute | solution.py:174
  602.3 3.1 collective-permute-start.3
  605.4 2.8 fusion.36
  608.2 2.9 fusion.37
  612.1 151.6 %collective-permute-done.3 = f32[1,256,2048]{2,1,0:T(8,128)} collective-permute-done((f32[1,256,2048]{2,1,0:T(8,128)}, f32[1,256,2048]{2,1,0:T(8,128)}, u32[]{:S(2)}, u32[]{:S(2)}) %collective-permute-start.3) | collective-permute-done | bytes 2097184 | tf_op jit(solution)/shard_map/ppermute | solution.py:174
  763.7 4.1 multiply_reduce_fusion
  767.9 9.1 multiply_add_fusion.1
  780.8 8.7 fusion.3
  789.6 5.6 fusion.62
  797.7 8.9 fusion
  806.6 5.5 fusion.65
  812.2 6.8 fusion.16
  822.1 7.0 fusion.17
  838.9 2.1 fusion.196
  841.0 2.8 reduce-scatter.10.cloned.1.call-done
  844.7 23.9 %reduce-scatter.12.cloned.1.call-done = f32[256,128]{0,1:T(8,128)} async-done(((f32[1024,128]{0,1:T(8,128)}), f32[256,128]{0,1:T(8,128)}) %reduce-scatter.12.cloned.1.call-update) | async-done | bytes 131088 | tf_op jit(solution)/shard_map/reduce_scatter | solution.py:210
  870.3 2.1 convolution_add_fusion.6
  883.4 2.9 convolution_add_fusion.4
  887.2 2.5 fusion.79
  889.7 2.7 convolution_add_fusion.3
  892.7 3.4 fusion.199
  896.1 6.1 convolution_add_fusion.2
  902.3 3.3 fusion.200
  905.6 6.1 convolution_add_fusion.1
  912.9 3.1 fusion.82
  916.0 5.9 convolution_add_fusion
  923.8 2.7 pad_maximum_fusion.1
  926.6 105.7 %all-reduce.10.cloned.1.call-done = (f32[1,256,2048]{2,1,0:T(8,128)}, f32[1,256,2048]{2,1,0:T(8,128)}) async-done(((f32[1,256,2048]{2,1,0:T(8,128)}, f32[1,256,2048]{2,1,0:T(8,128)}), (f32[1,256,2048]{2,1,0:T(8,128)}, f32[1,256,2048]{2,1,0:T(8,128)})) %all-reduce.10.cloned.1.call-update) | async-done | bytes 4194320 | tf_op jit(solution)/shard_map/psum | solution.py:227
  1032.3 3.3 fusion.43
  1035.6 23.9 %all-reduce.2 = (f32[2048]{0:T(1024)S(1)}, f32[2048]{0:T(1024)S(1)}) all-reduce(f32[2048]{0:T(1024)S(1)} %add.272, f32[2048]{0:T(1024)S(1)} %add.277), channel_id=6, replica_groups=mesh['dp'=2,'ctx'=4,'tensor'=4] {'dp','ctx'}, use_global_device_ids=true, to_apply=%region_24.25.clone | all-reduce | flops 4096 | bytes 32768
  1060.8 4.5 fusion.42
  1065.4 2.5 pad_maximum_fusion
  1069.1 37.7 %reduce-scatter.18.cloned.1.call-done = f32[256,64]{0,1:T(8,128)} async-done(((f32[2048,64]{0,1:T(8,128)}), f32[256,64]{0,1:T(8,128)}) %reduce-scatter.18.cloned.1.call-update) | async-done | bytes 65552 | tf_op jit(solution)/shard_map/reduce_scatter | solution.py:236
  1106.7 55.1 %reduce-scatter.14.cloned.1.call-done = f32[256,512]{1,0:T(8,128)} async-done(((f32[2048,512]{1,0:T(8,128)}), f32[256,512]{1,0:T(8,128)}) %reduce-scatter.14.cloned.1.call-update) | async-done | bytes 524304 | tf_op jit(solution)/shard_map/reduce_scatter | solution.py:234
  1161.9 54.9 %reduce-scatter.20.cloned.1.call-done = f32[512,256]{1,0:T(8,128)} async-done(((f32[512,2048]{1,0:T(8,128)}), f32[512,256]{1,0:T(8,128)}) %reduce-scatter.20.cloned.1.call-update) | async-done | bytes 524304 | tf_op jit(solution)/shard_map/reduce_scatter | solution.py:237
  1216.8 91.1 %reduce-scatter.22.cloned.1.call-done = f32[256,1408]{1,0:T(8,128)} async-done(((f32[2048,1408]{1,0:T(8,128)}), f32[256,1408]{1,0:T(8,128)}) %reduce-scatter.22.cloned.1.call-update) | async-done | bytes 1441808 | tf_op jit(solution)/shard_map/reduce_scatter | solution.py:239
  1307.8 91.1 %reduce-scatter.24.cloned.1.call-done = f32[256,1408]{1,0:T(8,128)} async-done(((f32[2048,1408]{1,0:T(8,128)}), f32[256,1408]{1,0:T(8,128)}) %reduce-scatter.24.cloned.1.call-update) | async-done | bytes 1441808 | tf_op jit(solution)/shard_map/reduce_scatter | solution.py:240
  1398.9 90.8 %reduce-scatter.26.cloned.1.call-done = f32[1408,256]{1,0:T(8,128)} async-done(((f32[1408,2048]{1,0:T(8,128)}), f32[1408,256]{1,0:T(8,128)}) %reduce-scatter.26.cloned.1.call-update) | async-done | bytes 1441808 | tf_op jit(solution)/shard_map/reduce_scatter | solution.py:241
  (312 shorter events, 79.1 us)
Async XLA Ops:
  7.2 24.7 %copy-start.2 = (bf16[2,256,2048]{2,1,0:T(8,128)(2,1)S(1)}, bf16[2,256,2048]{2,1,0:T(8,128)(2,1)}, u32[]{:S(2)}) copy-start(bf16[2,256,2048]{2,1,0:T(8,128)(2,1)} %param.12) | copy-start | bytes 6291460
  7.2 14.8 copy-start.79
  7.2 71.7 %all-gather.10.cloned.1.call-start = ((), (), s32[]{:S(2)}) async-start(), calls=%async_computation.9 | async-start | bytes 2359296 | tf_op jit(solution)/shard_map/all_gather | solution.py:47
  7.9 87.7 %all-gather.12.cloned.1.call-start = ((), (), s32[]{:S(2)}) async-start(), calls=%async_computation.10 | async-start | bytes 2359296 | tf_op jit(solution)/shard_map/all_gather | solution.py:50
  8.7 248.4 %all-reduce.12.cloned.1.call-start = ((), (), s32[]{:S(2)}) async-start(), calls=%async_computation.24 | async-start | bytes 8388608 | tf_op jit(solution)/shard_map/psum | solution.py:148
  8.7 35.8 %copy-start.88 = (f32[32]{0:T(128)}, f32[32]{0:T(128)S(1)}, u32[]{:S(2)}) copy-start(f32[32]{0:T(128)S(1)} %multiply_power_fusion) | copy-start | bytes 388
  8.8 35.8 %copy-start.86 = (f32[256]{0:T(256)}, f32[256]{0:T(256)S(1)}, u32[]{:S(2)}) copy-start(f32[256]{0:T(256)S(1)} %fusion.169) | copy-start | bytes 3076
  22.0 60.9 %copy-start.82 = (f32[256]{0:T(256)}, f32[256]{0:T(256)S(1)}, u32[]{:S(2)}) copy-start(f32[256]{0:T(256)S(1)} %add_rsqrt_fusion.3) | copy-start | bytes 3076
  22.0 63.4 %copy-start.84 = (f32[256]{0:T(256)}, f32[256]{0:T(256)S(1)}, u32[]{:S(2)}) copy-start(f32[256]{0:T(256)S(1)} %add_rsqrt_fusion.1) | copy-start | bytes 3076
  43.2 7.0 copy-start.90
  66.4 25.2 %copy-start.56 = (bf16[1024,64]{0,1:T(8,128)(2,1)}, bf16[1024,64]{0,1:T(8,128)(2,1)S(1)}, u32[]{:S(2)}) copy-start(bf16[1024,64]{0,1:T(8,128)(2,1)S(1)} %all-gather.1) | copy-start | bytes 393220
  71.9 16.0 %copy-start.32 = (bf16[1,1024,64]{1,2,0:T(8,128)(2,1)}, bf16[1,1024,64]{1,2,0:T(8,128)(2,1)S(1)}, u32[]{:S(2)}) copy-start(bf16[1,1024,64]{1,2,0:T(8,128)(2,1)S(1)} %all_gather.59) | copy-start | bytes 393220
  87.9 3.7 copy-start
  87.9 3.7 copy-start.67
  89.4 4.6 copy-start.1
  95.6 3.8 copy-start.42
  95.6 3.8 copy-start.5
  101.5 199.5 %all-gather.14.cloned.1.call-start = ((), (), s32[]{:S(2)}) async-start(), calls=%async_computation.11 | async-start | bytes 6488064 | tf_op jit(solution)/shard_map/all_gather | solution.py:52
  102.1 243.9 %all-gather.16.cloned.1.call-start = ((), (), s32[]{:S(2)}) async-start(), calls=%async_computation.12 | async-start | bytes 6488064 | tf_op jit(solution)/shard_map/all_gather | solution.py:53
  102.7 289.3 %all-gather.18.cloned.1.call-start = ((), (), s32[]{:S(2)}) async-start(), calls=%async_computation.13 | async-start | bytes 6488064 | tf_op jit(solution)/shard_map/all_gather | solution.py:54
  103.2 664.6 %all-reduce.14.cloned.1.call-start = ((), (), s32[]{:S(2)}) async-start(), calls=%async_computation.25 | async-start | bytes 4194304 | tf_op jit(solution)/shard_map/psum | solution.py:157
  262.7 83.3 %copy-start.16 = (bf16[256,2048]{1,0:T(8,128)(2,1)}, bf16[256,2048]{1,0:T(8,128)(2,1)S(1)}, u32[]{:S(2)}) copy-start(bf16[256,2048]{1,0:T(8,128)(2,1)S(1)} %fusion.72) | copy-start | bytes 3145732
  392.0 6.2 copy-start.91
  398.2 207.2 %copy-start.48 = (bf16[256,1408]{1,0:T(8,128)(2,1)}, bf16[256,1408]{1,0:T(8,128)(2,1)S(1)}, u32[]{:S(2)}) copy-start(bf16[256,1408]{1,0:T(8,128)(2,1)S(1)} %get-tuple-element.37) | copy-start | bytes 2162692
  398.2 3.4 copy-start.92
  400.1 54.0 %slice-start = ((s8[5767168]{0:T(1024)(128)(4,1)}), s8[4194304]{0:T(1024)(128)(4,1)S(1)}, s32[]{:S(2)}) async-start(s8[5767168]{0:T(1024)(128)(4,1)} %bitcast.376), calls=%async_computation.26 | async-start | bytes 8388608
  401.6 52.5 %slice-start.1 = ((s8[5767168]{0:T(1024)(128)(4,1)}), s8[1572864]{0:T(1024)(128)(4,1)S(1)}, s32[]{:S(2)}) async-start(s8[5767168]{0:T(1024)(128)(4,1)} %bitcast.376), calls=%async_computation.27 | async-start | bytes 3145728
  403.4 50.6 %copy-start.17 = (bf16[2,256,2048]{2,1,0:T(8,128)(2,1)S(1)}, bf16[2,256,2048]{2,1,0:T(8,128)(2,1)}, u32[]{:S(2)}) copy-start(bf16[2,256,2048]{2,1,0:T(8,128)(2,1)} %param.13) | copy-start | bytes 6291460
  403.5 47.8 %collective-permute-start = (f32[1,256,2048]{2,1,0:T(8,128)S(1)}, f32[1,256,2048]{2,1,0:T(8,128)S(1)}, u32[]{:S(2)}, u32[]{:S(2)}) collective-permute-start(f32[1,256,2048]{2,1,0:T(8,128)S(1)} %fusion.35), channel_id=1, source_target_pairs={{0,1},{1,0},{2,3},{3,2},{4,5},{5,4},{6,7},{7,6},{8,9},{9,8},{10,11... | collective-permute-start | bytes 6291464 | tf_op jit(solution)/shard_map/ppermute | solution.py:174
  451.6 92.8 %copy-start.14 = (f32[1,256,2048]{2,1,0:T(8,128)}, f32[1,256,2048]{2,1,0:T(8,128)S(1)}, u32[]{:S(2)}) copy-start(f32[1,256,2048]{2,1,0:T(8,128)S(1)} %add.249) | copy-start | bytes 6291460
  451.6 92.8 %collective-permute-start.1 = (f32[1,256,2048]{2,1,0:T(8,128)S(1)}, f32[1,256,2048]{2,1,0:T(8,128)S(1)}, u32[]{:S(2)}, u32[]{:S(2)}) collective-permute-start(f32[1,256,2048]{2,1,0:T(8,128)S(1)} %add.249), channel_id=1, source_target_pairs={{0,2},{1,3},{2,0},{3,1},{4,6},{5,7},{6,4},{7,5},{8,10},{9,11},{10,... | collective-permute-start | bytes 6291464 | tf_op jit(solution)/shard_map/ppermute | solution.py:174
  454.1 90.3 %copy-start.10 = (f32[1,256,2048]{2,1,0:T(8,128)S(1)}, f32[1,256,2048]{2,1,0:T(8,128)}, u32[]{:S(2)}) copy-start(f32[1,256,2048]{2,1,0:T(8,128)} %copy-done.9) | copy-start | bytes 6291460
  454.1 90.3 %copy-start.11 = (f32[1,256,2048]{2,1,0:T(8,128)S(1)}, f32[1,256,2048]{2,1,0:T(8,128)}, u32[]{:S(2)}) copy-start(f32[1,256,2048]{2,1,0:T(8,128)} %get-tuple-element.48) | copy-start | bytes 6291460
  550.3 57.9 %copy-start.22 = (bf16[256,1408]{1,0:T(8,128)(2,1)}, bf16[256,1408]{1,0:T(8,128)(2,1)S(1)}, u32[]{:S(2)}) copy-start(bf16[256,1408]{1,0:T(8,128)(2,1)S(1)} %get-tuple-element.40) | copy-start | bytes 2162692
  554.0 46.7 %collective-permute-start.2 = (f32[1,256,2048]{2,1,0:T(8,128)S(1)}, f32[1,256,2048]{2,1,0:T(8,128)S(1)}, u32[]{:S(2)}, u32[]{:S(2)}) collective-permute-start(f32[1,256,2048]{2,1,0:T(8,128)S(1)} %fusion.34), channel_id=1, source_target_pairs={{0,1},{1,0},{2,3},{3,2},{4,5},{5,4},{6,7},{7,6},{8,9},{9,8},{10,11... | collective-permute-start | bytes 6291464 | tf_op jit(solution)/shard_map/ppermute | solution.py:174
  602.3 161.4 %collective-permute-start.3 = (f32[1,256,2048]{2,1,0:T(8,128)}, f32[1,256,2048]{2,1,0:T(8,128)}, u32[]{:S(2)}, u32[]{:S(2)}) collective-permute-start(f32[1,256,2048]{2,1,0:T(8,128)} %add.262), channel_id=1, source_target_pairs={{0,2},{1,3},{2,0},{3,1},{4,6},{5,7},{6,4},{7,5},{8,10},{9,11},{10,... | collective-permute-start | bytes 6291464 | tf_op jit(solution)/shard_map/ppermute | solution.py:174
  611.0 232.8 %reduce-scatter.10.cloned.1.call-start = ((), (), s32[]{:S(2)}) async-start(), calls=%async_computation.14 | async-start | bytes 655360 | tf_op jit(solution)/shard_map/reduce_scatter | solution.py:210
  767.9 10.4 copy-start.6
  780.8 8.7 copy-start.60
  789.5 5.6 copy-start.7
  789.6 5.6 copy-start.12
  806.6 5.5 copy-start.61
  806.6 5.5 copy-start.77
  812.2 6.8 copy-start.39
  812.2 6.8 copy-start.41
  821.9 46.7 %reduce-scatter.12.cloned.1.call-start = ((), (), s32[]{:S(2)}) async-start(), calls=%async_computation.15 | async-start | bytes 655360 | tf_op jit(solution)/shard_map/reduce_scatter | solution.py:210
  822.1 7.1 copy-start.35
  822.1 7.1 copy-start.37
  834.9 197.4 %all-reduce.10.cloned.1.call-start = ((), (), s32[]{:S(2)}) async-start(), calls=%async_computation.23 | async-start | bytes 8388608 | tf_op jit(solution)/shard_map/psum | solution.py:227
  838.9 30.6 %copy-start.87 = (f32[256]{0:T(256)S(1)}, f32[256]{0:T(256)}, u32[]{:S(2)}) copy-start(f32[256]{0:T(256)} %copy-done.86) | copy-start | bytes 3076
  838.9 30.6 %copy-start.89 = (f32[32]{0:T(128)S(1)}, f32[32]{0:T(128)}, u32[]{:S(2)}) copy-start(f32[32]{0:T(128)} %copy-done.88) | copy-start | bytes 388
  838.9 31.4 %copy-start.25 = (bf16[2048,64]{0,1:T(8,128)(2,1)S(1)}, bf16[2048,64]{0,1:T(8,128)(2,1)}, u32[]{:S(2)}) copy-start(bf16[2048,64]{0,1:T(8,128)(2,1)} %copy-done.24) | copy-start | bytes 786436
  869.7 4.5 copy-start.73
  869.7 4.5 copy-start.75
  877.1 191.9 %reduce-scatter.16.cloned.1.call-start = ((), (), s32[]{:S(2)}) async-start(), calls=%async_computation.17 | async-start | bytes 589824 | tf_op jit(solution)/shard_map/reduce_scatter | solution.py:235
  879.6 227.1 %reduce-scatter.18.cloned.1.call-start = ((), (), s32[]{:S(2)}) async-start(), calls=%async_computation.18 | async-start | bytes 589824 | tf_op jit(solution)/shard_map/reduce_scatter | solution.py:236
  881.5 280.4 %reduce-scatter.14.cloned.1.call-start = ((), (), s32[]{:S(2)}) async-start(), calls=%async_computation.16 | async-start | bytes 4718592 | tf_op jit(solution)/shard_map/reduce_scatter | solution.py:234
  886.3 330.5 %reduce-scatter.20.cloned.1.call-start = ((), (), s32[]{:S(2)}) async-start(), calls=%async_computation.19 | async-start | bytes 4718592 | tf_op jit(solution)/shard_map/reduce_scatter | solution.py:237
  892.4 415.4 %reduce-scatter.22.cloned.1.call-start = ((), (), s32[]{:S(2)}) async-start(), calls=%async_computation.20 | async-start | bytes 12976128 | tf_op jit(solution)/shard_map/reduce_scatter | solution.py:239
  892.7 3.4 copy-start.55
  902.2 496.7 %reduce-scatter.24.cloned.1.call-start = ((), (), s32[]{:S(2)}) async-start(), calls=%async_computation.21 | async-start | bytes 12976128 | tf_op jit(solution)/shard_map/reduce_scatter | solution.py:240
  902.3 3.3 copy-start.53
  911.8 4.2 copy-start.23
  911.8 577.9 %reduce-scatter.26.cloned.1.call-start = ((), (), s32[]{:S(2)}) async-start(), calls=%async_computation.22 | async-start | bytes 12976128 | tf_op jit(solution)/shard_map/reduce_scatter | solution.py:241
  (54 other events, 86.1 us)
Sparse Core Ops, SparseCore 0:
  9.9 31.1 all-gather.9
  43.0 28.4 all-gather.11
  101.6 155.3 all-reduce.11
  258.8 42.1 all-gather.13
  302.7 43.1 all-gather.15
  347.7 44.2 all-gather.17
  611.2 152.3 all-reduce.13
  822.0 21.8 reduce-scatter.9
  846.9 21.6 reduce-scatter.11
  877.2 155.0 all-reduce.9
  1035.9 33.0 reduce-scatter.15
  1072.6 34.1 reduce-scatter.17
  1110.7 51.1 reduce-scatter.13
  1165.6 51.0 reduce-scatter.19
  1220.7 87.1 reduce-scatter.21
  1311.8 87.1 reduce-scatter.23
  1402.9 86.8 reduce-scatter.25
